TPU v7x, 32 devices: a whole 2x2x4 slice. The times are simulated.
32 devices in a mesh: bunch: 4 (over y, x), mp: 8 (over z, core).
Axes of the slice: x: 2, y: 2, z: 4, core: 2. Of those that a mesh axis runs over, the one named last changes fastest.
Arguments:
- phase_space: float32 [4, 64, 32768], P(None, 'bunch', 'mp')
- phase_advance: float32 [2, 64], P(None, 'bunch'), may hold values from 0.3 to 2.8
- centroid_history: float32 [2, 64, 64], P(None, None, 'bunch'), may hold values from -6 to 6
- lr_wake: float32 [4160], replicated, may hold values from -0.09375 to 0.09375
- sr_dipole: float32 [256, 256], replicated, may hold values from -24 to 24
- sr_quad: float32 [256, 256], replicated, may hold values from -24 to 24
- slice_ids: int32 [2, 64, 32768], P(None, 'bunch', 'mp'), may hold values from 0 to 255
Outputs:
- tracked: float32 [4, 64, 32768], P(None, 'bunch', 'mp')
- centroids: float32 [2, 2, 64], P(None, None, 'bunch')
All inputs are finite; a program needn't handle non-finite values.
Results may differ from a plain program's by a relative error of at most 0.00019.
Values sent between devices are 32-bit elements; how exact they have to be, the bound alone decides.
No kernel may reach another device: no remote copies, remote signals or barrier semaphores. Data moves between devices by JAX's collectives and lax.ppermute only.
A program may use at most 64 MiB of HBM per device.

v0:
```python
import jax
import jax.numpy as jnp
from jax import lax
from jax.sharding import PartitionSpec as P

SLICES = 256
TURNS = 2
DETUNE = 0.02


def body(phase_space, phase_advance, centroid_history, lr_wake, sr_dipole, sr_quad, slice_ids):
    highest = lax.Precision.HIGHEST
    bunch_dev = phase_space.shape[1]
    depth = centroid_history.shape[1]
    macro_total = phase_space.shape[2] * lax.axis_size("mp")
    all_bunches = bunch_dev * lax.axis_size("bunch")
    length = (depth + 1) * all_bunches
    offset_bunch = lax.axis_index("bunch") * bunch_dev
    own_index = jnp.arange(bunch_dev, dtype=jnp.int32)
    levels = jnp.arange(SLICES, dtype=jnp.int32)
    padded = jnp.concatenate([jnp.zeros((all_bunches,), jnp.float32), lr_wake])
    windows = jax.vmap(lambda start_at: lax.dynamic_slice(padded, (start_at,), (length,)))(
        offset_bunch + own_index
    )
    history = centroid_history
    whole = lax.all_gather(centroid_history, "bunch", axis=2, tiled=True)

    def moments_of(member):
        slice_line, line_x, line_y = member
        onehot = (slice_line[:, None] == levels[None, :]).astype(jnp.float32)
        stacked = jnp.stack([jnp.ones_like(line_x), line_x, line_y])
        return jnp.dot(stacked, onehot, precision=highest, preferred_element_type=jnp.float32)

    def lookup(member):
        slice_line, kick_rows = member
        onehot = (slice_line[:, None] == levels[None, :]).astype(jnp.float32)
        return lax.dot_general(
            kick_rows,
            onehot,
            (((1,), (1,)), ((), ())),
            precision=highest,
            preferred_element_type=jnp.float32,
        )

    coords = phase_space
    centroid_rows = []
    for turn_index in range(TURNS):
        slice_row = slice_ids[turn_index]
        moments = lax.map(moments_of, (slice_row, coords[0], coords[2]))
        moments = lax.psum(moments, "mp")
        density = moments[:, 0] / macro_total
        dipole = jnp.stack([moments[:, 1], moments[:, 2]]) / macro_total
        centroid = jnp.sum(dipole, axis=2)
        centroid_rows.append(centroid)
        dip_kick = jnp.einsum("pbj,ij->pbi", dipole, sr_dipole, precision=highest)
        quad_kick = jnp.einsum("bj,ij->bi", density, sr_quad, precision=highest)
        current_all = lax.all_gather(centroid, "bunch", axis=1, tiled=True)
        all_rows = jnp.concatenate([current_all[:, None, :], whole], axis=1)[:, :, ::-1].reshape(
            2, length
        )
        far_kick = jnp.einsum("bk,pk->pb", windows, all_rows, precision=highest)
        whole = jnp.concatenate([current_all[:, None, :], whole[:, :-1]], axis=1)
        kick_table = jnp.stack([dip_kick[0], dip_kick[1], quad_kick], axis=1)
        picked = lax.map(lookup, (slice_row, kick_table))
        coord_x, moment_x, coord_y, moment_y = (coords[0], coords[1], coords[2], coords[3])
        moment_x = moment_x + picked[:, 0] + picked[:, 2] * coord_x + far_kick[0][:, None]
        moment_y = moment_y + picked[:, 1] - picked[:, 2] * coord_y + far_kick[1][:, None]
        action = coord_x * coord_x + moment_x * moment_x + coord_y * coord_y + moment_y * moment_y
        angle_x = phase_advance[0][:, None] + DETUNE * action
        angle_y = phase_advance[1][:, None] + DETUNE * action
        new_x = jnp.cos(angle_x) * coord_x + jnp.sin(angle_x) * moment_x
        new_mx = -jnp.sin(angle_x) * coord_x + jnp.cos(angle_x) * moment_x
        new_y = jnp.cos(angle_y) * coord_y + jnp.sin(angle_y) * moment_y
        new_my = -jnp.sin(angle_y) * coord_y + jnp.cos(angle_y) * moment_y
        coords = jnp.stack([new_x, new_mx, new_y, new_my])
        history = jnp.concatenate([centroid[:, None, :], history[:, :-1]], axis=1)
    return (coords, jnp.stack(centroid_rows, axis=1))


def solution(mesh):
    placed = (
        P(None, "bunch", "mp"),
        P(None, "bunch"),
        P(None, None, "bunch"),
        P(),
        P(),
        P(),
        P(None, "bunch", "mp"),
    )
    return jax.shard_map(
        body,
        mesh=mesh,
        in_specs=placed,
        out_specs=(P(None, "bunch", "mp"), P(None, None, "bunch")),
        check_vma=False,
    )
```

profile of v0, /device:TPU:0, one launch (start us, length us, event | category | flops | bytes accessed | tf_op | source)
XLA Modules:
  0.0 306.1 jit_solution(7244623451006268379)
XLA Ops:
  1.6 9.9 %all_gather.10 = f32[2,64,64]{1,2,0:T(8,128)S(1)} all-gather(f32[2,64,16]{1,2,0:T(8,128)} %param.17), channel_id=1, replica_groups=mesh['bunch'=4,'mp'=8] {'bunch'}, dimensions={2}, use_global_device_ids=true | all-gather | bytes 40960 | tf_op jit(solution)/shard_map/all_gather | solution.py:26
  11.4 28.2 %while.45 = (s32[]{:T(128)}, f32[4224]{0:T(1024)S(1)}, s32[16,1]{0,1:T(1,128)S(1)}, f32[16,4160]{1,0:T(8,128)S(1)}, s32[]{:T(128)}, /*index=5*/s32[]{:T(128)}) while((s32[]{:T(128)}, f32[4224]{0:T(1024)S(1)}, s32[16,1]{0,1:T(1,128)S(1)}, f32[16,4160]{1,0:T(8,128)S(1)}, s32[]{:T(128)}, /*index=5*/s32[]{:T(128)}) %tuple.122), condition=%wide.while_cond, body=%wide.while_body.sunk | while | flops 2 | bytes 99937 | solution.py:22
  39.7 1.8 slice_bitcast_fusion
  41.5 25.6 %while.46 = (s32[]{:T(128)}, f32[16,3,256]{2,0,1:T(8,128)S(1)}, f32[16,4096]{1,0:T(8,128)S(1)}, f32[16,4096]{1,0:T(8,128)S(1)}, s32[16,4096]{1,0:T(8,128)S(1)}, ...) while((s32[]{:T(128)}, f32[16,3,256]{2,0,1:T(8,128)S(1)}, f32[16,4096]{1,0:T(8,128)S(1)}, ...), condition=%wide.region_1.2_spmd.clone, body=%wide.region_0.1_spmd.clone.sunk | while | flops 38821888 | bytes 162961 | solution.py:49
  41.6 1.4 fusion.77
  43.2 1.4 fusion.77
  44.8 1.4 fusion.77
  46.4 1.4 fusion.77
  48.0 1.4 fusion.77
  49.6 1.4 fusion.77
  51.2 1.4 fusion.77
  52.8 1.4 fusion.77
  54.4 1.4 fusion.77
  56.0 1.4 fusion.77
  57.6 1.4 fusion.77
  59.2 1.4 fusion.77
  60.8 1.4 fusion.77
  62.4 1.4 fusion.77
  64.0 1.4 fusion.77
  65.6 1.4 fusion.77
  67.1 27.5 %psum.14 = f32[16,3,256]{2,0,1:T(8,128)S(1)} all-reduce(f32[16,3,256]{2,0,1:T(8,128)S(1)} %get-tuple-element.120), channel_id=1, replica_groups=mesh['bunch'=4,'mp'=8] {'mp'}, use_global_device_ids=true, to_apply=%region_2.3 | all-reduce | flops 12288 | bytes 98304 | tf_op jit(solution)/shard_map/psum | solution.py:50
  95.5 7.7 %all-gather = f32[4,16,2]{1,2,0:T(2,128)S(1)} all-gather(f32[1,16,2]{1,2,0:T(2,128)S(1)} %bitcast.229), channel_id=1, replica_groups=mesh['bunch'=4,'mp'=8] {'bunch'}, dimensions={0}, use_global_device_ids=true | all-gather | bytes 640 | tf_op jit(solution)/shard_map/all_gather | solution.py:57
  104.2 42.7 %while.47 = (s32[]{:T(128)}, f32[16,3,4096]{2,0,1:T(8,128)S(1)}, f32[16,3,256]{2,0,1:T(8,128)S(1)}, s32[16,4096]{1,0:T(8,128)S(1)}, s32[]{:T(128)}, /*index=5*/s32[]{:T(128)}) while((s32[]{:T(128)}, f32[16,3,4096]{2,0,1:T(8,128)S(1)}, f32[16,3,256]{2,0,1:T(8,128)S(1)}, s32[16,4096]{1,0:T(8,128)S(1)}, s32[]{:T(128)}, ...), condition=%wide.region_4.5_spmd.clone, body=%wide.region_3.4_spmd.clone.sunk | while | flops 38797312 | bytes 304217 | solution.py:64
  104.3 2.1 convolution_bitcast_fusion.6
  107.0 2.1 convolution_bitcast_fusion.6
  109.6 2.1 convolution_bitcast_fusion.6
  112.3 2.1 convolution_bitcast_fusion.6
  115.0 2.1 convolution_bitcast_fusion.6
  117.6 2.1 convolution_bitcast_fusion.6
  120.3 2.1 convolution_bitcast_fusion.6
  123.0 2.1 convolution_bitcast_fusion.6
  125.7 2.1 convolution_bitcast_fusion.6
  128.3 2.1 convolution_bitcast_fusion.6
  131.0 2.1 convolution_bitcast_fusion.6
  133.7 2.1 convolution_bitcast_fusion.6
  136.3 2.1 convolution_bitcast_fusion.6
  139.0 2.1 convolution_bitcast_fusion.6
  141.7 2.1 convolution_bitcast_fusion.6
  144.3 2.1 convolution_bitcast_fusion.6
  147.0 3.1 %multiply_add_fusion.5 = (f32[16,4096]{1,0:T(8,128)}, f32[16,4096]{1,0:T(8,128)}) fusion(f32[16]{0:T(128)S(1)} %get-tuple-element.281, f32[16]{0:T(128)S(1)} %get-tuple-element.285, f32[16,3,4096]{2,0,1:T(8,128)S(1)} %get-tuple-element.121, f32[4,16,4096]{2,1,0:T(8,128)S(1)} %copy-done.1, f32[16]{0:T(128)S(1)} %get-tuple-element.286, ...), kind=kLoop, calls=%fused_computation.81 | loop fusion | flops 1572864 | bytes 2359552 | tf_op jit(solution)/shard_map/add | solution.py:73
  150.9 55.3 %while.48 = (s32[]{:T(128)}, f32[16,3,256]{2,0,1:T(8,128)S(1)}, f32[16,4096]{1,0:T(8,128)}, f32[16,4096]{1,0:T(8,128)}, s32[16,4096]{1,0:T(8,128)}, /*index=5*/s32[]{:T(128)}, f32[]{:T(128)}, f32[]{:T(128)}, s32[]{:T(128)}) while((s32[]{:T(128)}, f32[16,3,256]{2,0,1:T(8,128)S(1)}, f32[16,4096]{1,0:T(8,128)}, f32[16,4096]{1,0:T(8,128)}, ...), condition=%wide.region_7.8_spmd.clone, body=%wide.region_6.7_spmd.clone.sunk | while | flops 38821888 | bytes 162961 | solution.py:49
  187.5 1.4 fusion.79
  190.9 1.4 fusion.79
  206.3 26.3 %psum.15 = f32[16,3,256]{2,0,1:T(8,128)S(1)} all-reduce(f32[16,3,256]{2,0,1:T(8,128)S(1)} %get-tuple-element.122), channel_id=1, replica_groups=mesh['bunch'=4,'mp'=8] {'mp'}, use_global_device_ids=true, to_apply=%region_8.9 | all-reduce | flops 12288 | bytes 98304 | tf_op jit(solution)/shard_map/psum | solution.py:50
  234.0 7.5 %all-gather.1 = f32[4,16,2]{1,2,0:T(2,128)S(1)} all-gather(f32[1,16,2]{1,2,0:T(2,128)S(1)} %bitcast.232), channel_id=1, replica_groups=mesh['bunch'=4,'mp'=8] {'bunch'}, dimensions={0}, use_global_device_ids=true | all-gather | bytes 640 | tf_op jit(solution)/shard_map/all_gather | solution.py:57
  242.5 57.1 %while.49 = (s32[]{:T(128)}, f32[16,3,4096]{2,0,1:T(8,128)S(1)}, f32[16,3,256]{2,0,1:T(8,128)S(1)}, s32[16,4096]{1,0:T(8,128)}, s32[]{:T(128)}, /*index=5*/s32[]{:T(128)}) while((s32[]{:T(128)}, f32[16,3,4096]{2,0,1:T(8,128)S(1)}, f32[16,3,256]{2,0,1:T(8,128)S(1)}, s32[16,4096]{1,0:T(8,128)}, s32[]{:T(128)}, ...), condition=%wide.region_10.11_spmd.clone, body=%wide.region_9.10_spmd.clone.sunk | while | flops 38797312 | bytes 304217 | solution.py:64
  243.5 2.1 convolution_bitcast_fusion.7
  247.0 2.1 convolution_bitcast_fusion.7
  250.6 2.1 convolution_bitcast_fusion.7
  254.2 2.1 convolution_bitcast_fusion.7
  257.8 2.1 convolution_bitcast_fusion.7
  261.3 2.1 convolution_bitcast_fusion.7
  264.9 2.1 convolution_bitcast_fusion.7
  268.5 2.1 convolution_bitcast_fusion.7
  272.0 2.1 convolution_bitcast_fusion.7
  275.6 2.1 convolution_bitcast_fusion.7
  279.2 2.1 convolution_bitcast_fusion.7
  282.7 2.1 convolution_bitcast_fusion.7
  286.3 2.1 convolution_bitcast_fusion.7
  289.9 2.1 convolution_bitcast_fusion.7
  293.4 2.1 convolution_bitcast_fusion.7
  297.0 2.1 convolution_bitcast_fusion.7
  299.6 3.3 %multiply_add_fusion.3 = (f32[1,16,4096]{2,1,0:T(8,128)S(1)}, f32[1,16,4096]{2,1,0:T(8,128)S(1)}, f32[1,16,4096]{2,1,0:T(8,128)S(1)}, f32[1,16,4096]{2,1,0:T(8,128)S(1)}, f32[1,16,4096]{2,1,0:T(8,128)S(1)}) fusion(f32[16]{0:T(128)S(1)} %copy-done.4, f32[16]{0:T(128)S(1)} %get-tuple-element.280, f32[16,3,4096]{2,0,1:T(8,128)S(1)} %get-tuple-element.123, ...), kind=kLoop, calls=%fused_computation.77 | loop fusion | flops 2359296 | bytes 3408128 | tf_op jit(solution)/shard_map/add | solution.py:71
  302.9 2.2 multiply_add_fusion.1
  (424 shorter events, 118.6 us)
Async XLA Ops:
  0.6 94.5 %copy-start = (f32[256,256]{1,0:T(8,128)S(1)}, f32[256,256]{1,0:T(8,128)}, u32[]{:S(2)}) copy-start(f32[256,256]{1,0:T(8,128)} %param.19) | copy-start | bytes 786436
  0.6 40.8 %copy-start.1 = (f32[4,16,4096]{2,1,0:T(8,128)S(1)}, f32[4,16,4096]{2,1,0:T(8,128)}, u32[]{:S(2)}) copy-start(f32[4,16,4096]{2,1,0:T(8,128)} %param.15) | copy-start | bytes 3145732
  41.5 53.2 %copy-start.2 = (f32[256,256]{1,0:T(8,128)S(1)}, f32[256,256]{1,0:T(8,128)}, u32[]{:S(2)}) copy-start(f32[256,256]{1,0:T(8,128)} %param.20) | copy-start | bytes 786436
  67.1 37.0 %copy-start.7 = (f32[2,16]{1,0:T(2,128)S(1)}, f32[2,16]{1,0:T(2,128)}, u32[]{:S(2)}) copy-start(f32[2,16]{1,0:T(2,128)} %param.16) | copy-start | bytes 388
  104.1 42.8 %copy-start.3 = (f32[16]{0:T(128)}, f32[16]{0:T(128)S(1)}, u32[]{:S(2)}) copy-start(f32[16]{0:T(128)S(1)} %get-tuple-element.282) | copy-start | bytes 196
  104.2 42.8 %copy-start.5 = (f32[16]{0:T(128)}, f32[16]{0:T(128)S(1)}, u32[]{:S(2)}) copy-start(f32[16]{0:T(128)S(1)} %get-tuple-element.285) | copy-start | bytes 196
  104.2 42.8 %copy-start.6 = (f32[16]{0:T(128)}, f32[16]{0:T(128)S(1)}, u32[]{:S(2)}) copy-start(f32[16]{0:T(128)S(1)} %get-tuple-element.286) | copy-start | bytes 196
  242.5 57.1 %copy-start.4 = (f32[16]{0:T(128)S(1)}, f32[16]{0:T(128)}, u32[]{:S(2)}) copy-start(f32[16]{0:T(128)} %copy-done.3) | copy-start | bytes 196
where the time goes:
time: 307 us; the launch traced here: 306 us
  matrix products  116 us (38%)
  local copies, waits for them, and re-layouts  95.8 us (31%)
  blocking collectives  78.9 us (26%)
  other arithmetic  10.8 us (4%)
  loops' own time  3.22 us (1%)
    dot_general x32, matrix products, lookup(): lax.dot_general(kick_rows, onehot, (((1,), (1,)), ((), ())), precision=hi...  68 us
    psum x2, blocking collectives, body(): moments = lax.psum(moments, 'mp')  53.9 us
    dynamic_slice x96, local copies, waits for them, and re-layouts, body(): moments = lax.map(moments_of, (slice_row, coords[0], coords[2]))  46.8 us
    dot_general x32, matrix products, moments_of(): jnp.dot(stacked, onehot, precision=highest, preferred_element_type=jnp.fl...  46.3 us
    gather x64, local copies, waits for them, and re-layouts  27.8 us
    all_gather x2, blocking collectives, body(): current_all = lax.all_gather(centroid, 'bunch', axis=1, tiled=True)  15.2 us
    dynamic_update_slice x64, local copies, waits for them, and re-layouts, body(): picked = lax.map(lookup, (slice_row, kick_table))  14.9 us
    all_gather x1, blocking collectives, body(): whole = lax.all_gather(centroid_history, 'bunch', axis=2, tiled=True)  9.87 us

commit v1 on v0

--- a/solution.py
+++ b/solution.py
@@ -47,7 +47,9 @@
     for turn_index in range(TURNS):
         slice_row = slice_ids[turn_index]
         moments = lax.map(moments_of, (slice_row, coords[0], coords[2]))
-        moments = lax.psum(moments, "mp")
+        moments = moments
+        for hop in (1, 2, 4):
+            moments = moments + lax.ppermute(moments, "mp", [(dev, dev ^ hop) for dev in range(8)])
         density = moments[:, 0] / macro_total
         dipole = jnp.stack([moments[:, 1], moments[:, 2]]) / macro_total
         centroid = jnp.sum(dipole, axis=2)

time: 307 us -> 241 us (0.79)
  blocking collectives: 78.9 us -> 23.6 us
  local copies, waits for them, and re-layouts: 95.8 us -> 66.9 us
  waiting for transfers between devices: 0 us -> 11.1 us
  starting transfers between devices: 0 us -> 8.75 us
    psum x2 -> x0, blocking collectives: 53.9 us -> none  [body(): moments = lax.psum(moments, 'mp')]
    dynamic_slice x96, local copies, waits for them, and re-layouts: 46.8 us -> 16.9 us  [body(): moments = lax.map(moments_of, (slice_row, coords[0], coords[2]))]
    ppermute x0 -> x6, waiting for transfers between devices: none -> 11.1 us  [body(): lax.ppermute(moments, 'mp', [(dev, dev ^ hop) for dev in range(8)])]
    ppermute x0 -> x6, starting transfers between devices: none -> 8.75 us  [body(): lax.ppermute(moments, 'mp', [(dev, dev ^ hop) for dev in range(8)])]
  transfers between devices with their start and end apart: 0 -> 6, of which waited for: 0 -> 5; matrix products, arithmetic and copies ran while one was open for 0% -> 12% of each run, Pallas kernels for 0% -> 0%
where the time goes in v1:
time: 241 us; the launch traced here: 240 us
  matrix products  116 us (48%)
  local copies, waits for them, and re-layouts  66.9 us (28%)
  blocking collectives  23.6 us (10%)
  waiting for transfers between devices  11.1 us (5%)
  other arithmetic  9.41 us (4%)
  starting transfers between devices  8.75 us (4%)
  loops' own time  3.35 us (1%)
    dot_general x32, matrix products, lookup(): lax.dot_general(kick_rows, onehot, (((1,), (1,)), ((), ())), precision=hi...  68 us
    dot_general x32, matrix products, moments_of(): jnp.dot(stacked, onehot, precision=highest, preferred_element_type=jnp.fl...  46.3 us
    gather x64, local copies, waits for them, and re-layouts  29.6 us
    dynamic_slice x96, local copies, waits for them, and re-layouts, body(): moments = lax.map(moments_of, (slice_row, coords[0], coords[2]))  16.9 us
    all_gather x2, blocking collectives, body(): current_all = lax.all_gather(centroid, 'bunch', axis=1, tiled=True)  15.3 us
    dynamic_update_slice x64, local copies, waits for them, and re-layouts, body(): picked = lax.map(lookup, (slice_row, kick_table))  15.1 us
    ppermute x6, waiting for transfers between devices, body(): lax.ppermute(moments, 'mp', [(dev, dev ^ hop) for dev in range(8)])  11.1 us
    ppermute x6, starting transfers between devices, body(): lax.ppermute(moments, 'mp', [(dev, dev ^ hop) for dev in range(8)])  8.75 us
  transfers between devices with their start and end apart: 6, of which 5 were waited for; matrix products, arithmetic and copies ran while one was open for 12% of the time, Pallas kernels for 0%

profile of v1, /device:TPU:0, one launch (start us, length us, event | category | flops | bytes accessed | tf_op | source)
XLA Modules:
  0.0 240.5 jit_solution(1176435010347008344)
XLA Ops:
  2.1 25.6 %while.46 = (s32[]{:T(128)}, f32[16,3,256]{2,0,1:T(8,128)S(1)}, f32[16,4096]{1,0:T(8,128)S(1)}, f32[16,4096]{1,0:T(8,128)S(1)}, s32[16,4096]{1,0:T(8,128)S(1)}, ...) while((s32[]{:T(128)}, f32[16,3,256]{2,0,1:T(8,128)S(1)}, f32[16,4096]{1,0:T(8,128)S(1)}, ...), condition=%wide.region_1.2_spmd.clone, body=%wide.region_0.1_spmd.clone.sunk | while | flops 38821888 | bytes 162961 | solution.py:49
  2.2 1.4 fusion.77
  3.8 1.4 fusion.77
  5.4 1.4 fusion.77
  7.0 1.4 fusion.77
  8.6 1.4 fusion.77
  10.2 1.4 fusion.77
  11.8 1.4 fusion.77
  13.4 1.4 fusion.77
  15.0 1.4 fusion.77
  16.6 1.4 fusion.77
  18.2 1.4 fusion.77
  19.8 1.4 fusion.77
  23.0 1.4 fusion.77
  29.2 3.0 %collective-permute-start.1 = (f32[16,3,256]{2,0,1:T(8,128)S(1)}, f32[16,3,256]{2,0,1:T(8,128)S(1)}, u32[]{:S(2)}, u32[]{:S(2)}) collective-permute-start(f32[16,3,256]{2,0,1:T(8,128)S(1)} %add.306), channel_id=1, source_target_pairs={{0,2},{1,3},{2,0},{3,1},{4,6},{5,7},{6,4},{7,5},{8,10},{9,11},{10,... | collective-permute-start | bytes 147464 | tf_op jit(solution)/shard_map/ppermute | solution.py:52
  32.2 2.1 collective-permute-done.1
  34.3 3.1 %collective-permute-start.2 = (f32[16,3,256]{2,0,1:T(8,128)S(1)}, f32[16,3,256]{2,0,1:T(8,128)S(1)}, u32[]{:S(2)}, u32[]{:S(2)}) collective-permute-start(f32[16,3,256]{2,0,1:T(8,128)S(1)} %add.307), channel_id=1, source_target_pairs={{0,4},{1,5},{2,6},{3,7},{4,0},{5,1},{6,2},{7,3},{8,12},{9,13},{10,... | collective-permute-start | bytes 147464 | tf_op jit(solution)/shard_map/ppermute | solution.py:52
  37.4 8.3 %all_gather.10 = f32[2,64,64]{1,2,0:T(8,128)S(1)} all-gather(f32[2,64,16]{1,2,0:T(8,128)S(1)} %copy-done.7), channel_id=1, replica_groups=mesh['bunch'=4,'mp'=8] {'bunch'}, dimensions={2}, use_global_device_ids=true | all-gather | bytes 40960 | tf_op jit(solution)/shard_map/all_gather | solution.py:26
  45.7 30.0 %while.45 = (s32[]{:T(128)}, f32[4224]{0:T(1024)S(1)}, s32[16,1]{0,1:T(1,128)S(1)}, f32[16,4160]{1,0:T(8,128)S(1)}, s32[]{:T(128)}, /*index=5*/s32[]{:T(128)}) while((s32[]{:T(128)}, f32[4224]{0:T(1024)S(1)}, s32[16,1]{0,1:T(1,128)S(1)}, f32[16,4160]{1,0:T(8,128)S(1)}, s32[]{:T(128)}, /*index=5*/s32[]{:T(128)}) %tuple.122), condition=%wide.while_cond, body=%wide.while_body.sunk | while | flops 2 | bytes 99937 | solution.py:22
  76.6 8.0 %all-gather = f32[4,16,2]{1,2,0:T(2,128)S(1)} all-gather(f32[1,16,2]{1,2,0:T(2,128)S(1)} %bitcast.229), channel_id=1, replica_groups=mesh['bunch'=4,'mp'=8] {'bunch'}, dimensions={0}, use_global_device_ids=true | all-gather | bytes 640 | tf_op jit(solution)/shard_map/all_gather | solution.py:59
  85.4 42.8 %while.47 = (s32[]{:T(128)}, f32[16,3,4096]{2,0,1:T(8,128)S(1)}, f32[16,3,256]{2,0,1:T(8,128)S(1)}, s32[16,4096]{1,0:T(8,128)S(1)}, s32[]{:T(128)}, /*index=5*/s32[]{:T(128)}) while((s32[]{:T(128)}, f32[16,3,4096]{2,0,1:T(8,128)S(1)}, f32[16,3,256]{2,0,1:T(8,128)S(1)}, s32[16,4096]{1,0:T(8,128)S(1)}, s32[]{:T(128)}, ...), condition=%wide.region_3.4_spmd.clone, body=%wide.region_2.3_spmd.clone.sunk | while | flops 38797312 | bytes 304217 | solution.py:66
  85.4 2.1 convolution_bitcast_fusion.6
  88.1 2.1 convolution_bitcast_fusion.6
  90.8 2.1 convolution_bitcast_fusion.6
  93.5 2.1 convolution_bitcast_fusion.6
  96.2 2.1 convolution_bitcast_fusion.6
  98.8 2.1 convolution_bitcast_fusion.6
  101.5 2.1 convolution_bitcast_fusion.6
  104.2 2.1 convolution_bitcast_fusion.6
  106.9 2.1 convolution_bitcast_fusion.6
  109.5 2.1 convolution_bitcast_fusion.6
  112.2 2.1 convolution_bitcast_fusion.6
  114.9 2.1 convolution_bitcast_fusion.6
  117.6 2.1 convolution_bitcast_fusion.6
  120.3 2.1 convolution_bitcast_fusion.6
  122.9 2.1 convolution_bitcast_fusion.6
  125.6 2.1 convolution_bitcast_fusion.6
  128.7 2.2 multiply_add_fusion.5
  130.9 25.6 %while.48 = (s32[]{:T(128)}, f32[16,3,256]{2,0,1:T(8,128)S(1)}, f32[16,4096]{1,0:T(8,128)S(1)}, f32[16,4096]{1,0:T(8,128)S(1)}, s32[16,4096]{1,0:T(8,128)S(1)}, ...) while((s32[]{:T(128)}, f32[16,3,256]{2,0,1:T(8,128)S(1)}, f32[16,4096]{1,0:T(8,128)S(1)}, ...), condition=%wide.region_6.7_spmd.clone, body=%wide.region_5.6_spmd.clone.sunk | while | flops 38821888 | bytes 162961 | solution.py:49
  139.0 1.4 fusion.79
  151.8 1.4 fusion.79
  157.8 1.6 collective-permute-start.4
  159.4 2.5 %collective-permute-done.4 = f32[16,3,256]{2,0,1:T(8,128)S(1)} collective-permute-done((f32[16,3,256]{2,0,1:T(8,128)S(1)}, f32[16,3,256]{2,0,1:T(8,128)S(1)}, u32[]{:S(2)}, u32[]{:S(2)}) %collective-permute-start.4) | collective-permute-done | bytes 49184 | tf_op jit(solution)/shard_map/ppermute | solution.py:52
  162.6 4.4 %collective-permute-done.5 = f32[16,3,256]{2,0,1:T(8,128)S(1)} collective-permute-done((f32[16,3,256]{2,0,1:T(8,128)S(1)}, f32[16,3,256]{2,0,1:T(8,128)S(1)}, u32[]{:S(2)}, u32[]{:S(2)}) %collective-permute-start.5) | collective-permute-done | bytes 49184 | tf_op jit(solution)/shard_map/ppermute | solution.py:52
  168.4 7.3 %all-gather.1 = f32[4,16,2]{1,2,0:T(2,128)S(1)} all-gather(f32[1,16,2]{1,2,0:T(2,128)S(1)} %bitcast.232), channel_id=1, replica_groups=mesh['bunch'=4,'mp'=8] {'bunch'}, dimensions={0}, use_global_device_ids=true | all-gather | bytes 640 | tf_op jit(solution)/shard_map/all_gather | solution.py:59
  176.8 57.2 %while.49 = (s32[]{:T(128)}, f32[16,3,4096]{2,0,1:T(8,128)S(1)}, f32[16,3,256]{2,0,1:T(8,128)S(1)}, s32[16,4096]{1,0:T(8,128)}, s32[]{:T(128)}, /*index=5*/s32[]{:T(128)}) while((s32[]{:T(128)}, f32[16,3,4096]{2,0,1:T(8,128)S(1)}, f32[16,3,256]{2,0,1:T(8,128)S(1)}, s32[16,4096]{1,0:T(8,128)}, s32[]{:T(128)}, ...), condition=%wide.region_8.9_spmd.clone, body=%wide.region_7.8_spmd.clone.sunk | while | flops 38797312 | bytes 304217 | solution.py:66
  177.7 2.1 convolution_bitcast_fusion.7
  181.3 2.1 convolution_bitcast_fusion.7
  184.9 2.1 convolution_bitcast_fusion.7
  188.4 2.1 convolution_bitcast_fusion.7
  192.0 2.1 convolution_bitcast_fusion.7
  195.6 2.1 convolution_bitcast_fusion.7
  199.2 2.1 convolution_bitcast_fusion.7
  202.7 2.1 convolution_bitcast_fusion.7
  206.3 2.1 convolution_bitcast_fusion.7
  209.9 2.1 convolution_bitcast_fusion.7
  213.5 2.1 convolution_bitcast_fusion.7
  217.0 2.1 convolution_bitcast_fusion.7
  220.6 2.1 convolution_bitcast_fusion.7
  224.2 2.1 convolution_bitcast_fusion.7
  227.8 2.1 convolution_bitcast_fusion.7
  231.4 2.1 convolution_bitcast_fusion.7
  234.0 3.3 %multiply_add_fusion.3 = (f32[1,16,4096]{2,1,0:T(8,128)S(1)}, f32[1,16,4096]{2,1,0:T(8,128)S(1)}, f32[1,16,4096]{2,1,0:T(8,128)S(1)}, f32[1,16,4096]{2,1,0:T(8,128)S(1)}, f32[1,16,4096]{2,1,0:T(8,128)S(1)}) fusion(f32[16]{0:T(128)S(1)} %get-tuple-element.282, f32[16]{0:T(128)S(1)} %get-tuple-element.280, f32[16,3,4096]{2,0,1:T(8,128)S(1)} %get-tuple-element.123, ...), kind=kLoop, calls=%fused_computation.77 | loop fusion | flops 2359296 | bytes 3408128 | tf_op jit(solution)/shard_map/add | solution.py:73
  237.3 2.2 multiply_add_fusion.1
  (442 shorter events, 98.4 us)
Async XLA Ops:
  0.6 75.6 %copy-start = (f32[256,256]{1,0:T(8,128)S(1)}, f32[256,256]{1,0:T(8,128)}, u32[]{:S(2)}) copy-start(f32[256,256]{1,0:T(8,128)} %param.19) | copy-start | bytes 786436
  0.6 1.4 copy-start.1
  2.1 35.2 %copy-start.6 = (f32[4160]{0:T(1024)S(1)}, f32[4160]{0:T(1024)}, u32[]{:S(2)}) copy-start(f32[4160]{0:T(1024)} %param.18) | copy-start | bytes 49924
  2.1 35.3 %copy-start.7 = (f32[2,64,16]{1,2,0:T(8,128)S(1)}, f32[2,64,16]{1,2,0:T(8,128)}, u32[]{:S(2)}) copy-start(f32[2,64,16]{1,2,0:T(8,128)} %param.17) | copy-start | bytes 24580
  27.7 48.0 %copy-start.2 = (f32[256,256]{1,0:T(8,128)S(1)}, f32[256,256]{1,0:T(8,128)}, u32[]{:S(2)}) copy-start(f32[256,256]{1,0:T(8,128)} %param.20) | copy-start | bytes 786436
  27.7 1.4 collective-permute-start
  29.2 5.0 %collective-permute-start.1 = (f32[16,3,256]{2,0,1:T(8,128)S(1)}, f32[16,3,256]{2,0,1:T(8,128)S(1)}, u32[]{:S(2)}, u32[]{:S(2)}) collective-permute-start(f32[16,3,256]{2,0,1:T(8,128)S(1)} %add.306), channel_id=1, source_target_pairs={{0,2},{1,3},{2,0},{3,1},{4,6},{5,7},{6,4},{7,5},{8,10},{9,11},{10,... | collective-permute-start | bytes 147464 | tf_op jit(solution)/shard_map/ppermute | solution.py:52
  34.3 41.5 %collective-permute-start.2 = (f32[16,3,256]{2,0,1:T(8,128)S(1)}, f32[16,3,256]{2,0,1:T(8,128)S(1)}, u32[]{:S(2)}, u32[]{:S(2)}) collective-permute-start(f32[16,3,256]{2,0,1:T(8,128)S(1)} %add.307), channel_id=1, source_target_pairs={{0,4},{1,5},{2,6},{3,7},{4,0},{5,1},{6,2},{7,3},{8,12},{9,13},{10,... | collective-permute-start | bytes 147464 | tf_op jit(solution)/shard_map/ppermute | solution.py:52
  84.8 0.6 copy-start.4
  85.2 43.4 %copy-start.8 = (f32[2,16]{1,0:T(2,128)S(1)}, f32[2,16]{1,0:T(2,128)}, u32[]{:S(2)}) copy-start(f32[2,16]{1,0:T(2,128)} %param.16) | copy-start | bytes 388
  156.5 5.5 %copy-start.3 = (s32[16,4096]{1,0:T(8,128)}, s32[16,4096]{1,0:T(8,128)S(1)}, u32[]{:S(2)}) copy-start(s32[16,4096]{1,0:T(8,128)S(1)} %get-tuple-element.540) | copy-start | bytes 786436
  156.5 1.3 collective-permute-start.3
  157.8 4.2 %collective-permute-start.4 = (f32[16,3,256]{2,0,1:T(8,128)S(1)}, f32[16,3,256]{2,0,1:T(8,128)S(1)}, u32[]{:S(2)}, u32[]{:S(2)}) collective-permute-start(f32[16,3,256]{2,0,1:T(8,128)S(1)} %add.342), channel_id=1, source_target_pairs={{0,2},{1,3},{2,0},{3,1},{4,6},{5,7},{6,4},{7,5},{8,10},{9,11},{10,... | collective-permute-start | bytes 147464 | tf_op jit(solution)/shard_map/ppermute | solution.py:52
  162.0 5.1 %collective-permute-start.5 = (f32[16,3,256]{2,0,1:T(8,128)S(1)}, f32[16,3,256]{2,0,1:T(8,128)S(1)}, u32[]{:S(2)}, u32[]{:S(2)}) collective-permute-start(f32[16,3,256]{2,0,1:T(8,128)S(1)} %add.343), channel_id=1, source_target_pairs={{0,4},{1,5},{2,6},{3,7},{4,0},{5,1},{6,2},{7,3},{8,12},{9,13},{10,... | collective-permute-start | bytes 147464 | tf_op jit(solution)/shard_map/ppermute | solution.py:52
  162.6 13.3 %copy-start.5 = (f32[2,1,64]{1,2,0:T(8,128)S(1)}, f32[2,1,64]{1,2,0:T(8,128)}, u32[]{:S(2)}) copy-start(f32[2,1,64]{1,2,0:T(8,128)} %copy-done.4) | copy-start | bytes 1540
